TPU v7x, 32 devices: a whole 2x2x4 slice. The times are simulated.
32 devices in a mesh: grid: 8 (over y, x, core), sub: 4 (over z).
Axes of the slice: x: 2, y: 2, z: 4, core: 2. Of those that a mesh axis runs over, the one named last changes fastest.
Arguments:
- grid_x: bfloat16 [65536, 512], P(('grid', 'sub')), may hold values from -6 to 6
- mesh_h: bfloat16 [2048, 512], P(('grid', 'sub')), may hold values from -6 to 6
- gain_grid: float32 [512], replicated, may hold values from 0.1 to 1.9
- gain_mesh: float32 [512], replicated, may hold values from 0.1 to 1.9
- w_query: bfloat16 [512, 512], replicated, may hold values from -0.25 to 0.25
- w_key: bfloat16 [512, 512], replicated, may hold values from -0.25 to 0.25
- w_value: bfloat16 [512, 512], replicated, may hold values from -0.25 to 0.25
- w_out: bfloat16 [512, 512], replicated, may hold values from -0.25 to 0.25
- edge_bias: float32 [2048, 384], P(('grid', 'sub')), may hold values from -9 to 300
- neighbours: int32 [2048, 96], P(('grid', 'sub')), may hold values from 0 to 767, as said below
- valid: int32 [2048, 96], P(('grid', 'sub')), may hold values from 0 to 1, as said below
- send_rows: int32 [32, 3, 4, 64], P(('grid', 'sub')), may hold values from 0 to 2047, as said below
- out_grad: bfloat16 [2048, 512], P(('grid', 'sub')), may hold values from -24 to 24
Outputs:
- mesh_out: bfloat16 [2048, 512], P(('grid', 'sub'))
- mesh_grad: bfloat16 [2048, 512], P(('grid', 'sub'))
- grid_grad: bfloat16 [65536, 512], P(('grid', 'sub'))
- weight_grads: float32 [4, 512, 512], replicated
Inputs may be any that keep to these rules, and one draw needn't show every extreme that they name: `send_rows`: for each source device, slab offset and destination sub index the 64 local rows are distinct; rows sent to the slab below (o = 0) lie in the lower half of the device's 2048 rows, rows sent to the slab above (o = 2) in the upper half. `neighbours`: a slot (o * 4 + s) * 64 + t names row t of what device s of slab g - o + 1 sends to the node's device; slots of slabs outside the grid are never named; the 96 entries of a node are distinct; some slots are named by no node. The first two edges of every node are valid.
All inputs are finite; a program needn't handle non-finite values.
Results may differ from a plain program's by a relative error of at most 0.009.
Values may be sent and summed in bfloat16 or wider, within the bound.
A program may use at most 128 MiB of HBM per device.

v0:
```python
import jax
import jax.numpy as jnp
from jax import lax
from jax.sharding import PartitionSpec as P

EPSILON = 1e-06
NEG_FILL = -1e30


def from_behind(block, axis, distance):
    devices = range(lax.axis_size(axis))
    route = [(i - distance, i) for i in devices if i - distance in devices]
    return lax.ppermute(block, axis, route)


def normalize(values_in, gain_row):
    widened = values_in.astype(jnp.float32)
    factor = lax.rsqrt(jnp.mean(widened * widened, axis=-1, keepdims=True) + EPSILON)
    return (widened, factor, (widened * factor * gain_row).astype(jnp.bfloat16))


def normalize_back(widened, factor, gain_row, upstream):
    scaled = gain_row * upstream
    inner_mean = jnp.mean(widened * scaled, axis=-1, keepdims=True)
    return factor * scaled - widened * factor**3 * inner_mean


def shards(
    grid_x,
    mesh_h,
    gain_grid,
    gain_mesh,
    w_query,
    w_key,
    w_value,
    w_out,
    edge_bias,
    neighbours,
    valid,
    send_rows,
    out_grad,
):
    point_count, model_width = grid_x.shape
    node_count = mesh_h.shape[0]
    sub_count = send_rows.shape[2]
    slots_per = send_rows.shape[3]
    block = sub_count * slots_per
    slot_count = 3 * block
    fanout = neighbours.shape[1]
    head_count = edge_bias.shape[1] // fanout
    head_width = model_width // head_count
    logit_scale = head_width ** (-0.5)
    w_pair = jnp.concatenate([w_key, w_value], axis=1)
    grid_wide, grid_factor, grid_normed = normalize(grid_x, gain_grid)
    flat_rows = send_rows[0].reshape(slot_count)
    send_match = flat_rows[:, None] == jnp.arange(point_count, dtype=jnp.int32)[None, :]
    send_onehot = send_match.astype(jnp.bfloat16)
    sent_normed = jnp.dot(send_onehot, grid_normed, preferred_element_type=jnp.float32).astype(
        jnp.bfloat16
    )
    packet = sent_normed.reshape(3, sub_count, slots_per, model_width)
    packet_width = packet.shape[3]
    mixed = lax.all_to_all(packet, "sub", split_axis=1, concat_axis=1, tiled=True).reshape(
        3, block, packet_width
    )
    pieces = []
    for offset in (0, 1, 2):
        piece = mixed[offset]
        if offset != 1:
            piece = from_behind(piece, "grid", offset - 1)
        pieces.append(piece)
    arrived = jnp.concatenate(pieces, axis=0)
    recv_pair = jnp.dot(arrived, w_pair, preferred_element_type=jnp.float32).astype(jnp.bfloat16)
    slot_onehot = (
        neighbours[:, :, None] == jnp.arange(slot_count, dtype=jnp.int32)[None, None, :]
    ).astype(jnp.bfloat16)
    edge_pair = jnp.einsum(
        "gjc,ce->gje", slot_onehot, recv_pair, preferred_element_type=jnp.float32
    ).astype(jnp.bfloat16)
    edge_keys = edge_pair[:, :, :model_width].reshape(node_count, fanout, head_count, head_width)
    edge_values = edge_pair[:, :, model_width:].reshape(node_count, fanout, head_count, head_width)
    mesh_wide, mesh_factor, mesh_normed = normalize(mesh_h, gain_mesh)
    queries = (
        jnp.dot(mesh_normed, w_query, preferred_element_type=jnp.float32) * logit_scale
    ).astype(jnp.bfloat16)
    query_head_rows = queries.reshape(node_count, head_count, head_width)
    score_matrix = jnp.einsum(
        "gip,gjip->gij", query_head_rows, edge_keys, preferred_element_type=jnp.float32
    ) + edge_bias.reshape(node_count, head_count, fanout)
    live_mask = (valid == 1)[:, None, :]
    row_peak = jnp.max(jnp.where(live_mask, score_matrix, NEG_FILL), axis=2, keepdims=True)
    exp_terms = jnp.exp(jnp.where(live_mask, score_matrix - row_peak, NEG_FILL))
    attn_probs = exp_terms / jnp.sum(exp_terms, axis=2, keepdims=True)
    probabilities_batch = attn_probs.astype(jnp.bfloat16)
    attended_rows = (
        jnp.einsum(
            "gij,gjik->gik", probabilities_batch, edge_values, preferred_element_type=jnp.float32
        )
        .reshape(node_count, model_width)
        .astype(jnp.bfloat16)
    )
    mesh_out = (
        mesh_wide + jnp.dot(attended_rows, w_out, preferred_element_type=jnp.float32)
    ).astype(jnp.bfloat16)
    grad_wo = jnp.einsum("md,me->de", attended_rows, out_grad, preferred_element_type=jnp.float32)
    att_grad = jnp.einsum("me,de->md", out_grad, w_out, preferred_element_type=jnp.float32).astype(
        jnp.bfloat16
    )
    head_gradient = att_grad.reshape(node_count, head_count, head_width)
    probability_gradient = jnp.einsum(
        "gip,gjip->gij", head_gradient, edge_values, preferred_element_type=jnp.float32
    )
    score_gradient = (
        attn_probs
        * (probability_gradient - jnp.sum(attn_probs * probability_gradient, axis=2, keepdims=True))
    ).astype(jnp.bfloat16)
    query_gradient = (
        (
            jnp.einsum(
                "gij,gjik->gik", score_gradient, edge_keys, preferred_element_type=jnp.float32
            )
            * logit_scale
        )
        .reshape(node_count, model_width)
        .astype(jnp.bfloat16)
    )
    dense_score_gradient = jnp.einsum(
        "gij,gjc->gic", score_gradient, slot_onehot, preferred_element_type=jnp.float32
    ).astype(jnp.bfloat16)
    dense_probabilities = jnp.einsum(
        "gij,gjc->gic", probabilities_batch, slot_onehot, preferred_element_type=jnp.float32
    ).astype(jnp.bfloat16)
    key_part = jnp.einsum(
        "uza,uzt->azt", dense_score_gradient, query_head_rows, preferred_element_type=jnp.float32
    ).reshape(slot_count, model_width)
    value_part = jnp.einsum(
        "uza,uzt->azt", dense_probabilities, head_gradient, preferred_element_type=jnp.float32
    ).reshape(slot_count, model_width)
    back_packet = (
        jnp.concatenate([key_part, value_part], axis=1)
        .astype(jnp.bfloat16)
        .reshape(3, block, 2 * model_width)
    )
    home_pieces = []
    for offset in (0, 1, 2):
        piece = back_packet[offset]
        if offset != 1:
            piece = from_behind(piece, "grid", 1 - offset)
        home_pieces.append(piece)
    home = jnp.stack(home_pieces)
    home = home.reshape(3, sub_count, slots_per, 2 * model_width)
    returned = lax.all_to_all(home, "sub", split_axis=1, concat_axis=1, tiled=True).reshape(
        slot_count, 2 * model_width
    )
    pair_grads = jnp.einsum("sd,se->de", sent_normed, returned, preferred_element_type=jnp.float32)
    slot_back = jnp.einsum("se,de->sd", returned, w_pair, preferred_element_type=jnp.float32)
    normed_grad = jnp.einsum(
        "sp,sd->pd",
        send_match.astype(jnp.float32),
        slot_back,
        precision=lax.Precision.HIGHEST,
        preferred_element_type=jnp.float32,
    )
    grid_grad = normalize_back(grid_wide, grid_factor, gain_grid, normed_grad).astype(jnp.bfloat16)
    grad_wq = jnp.einsum(
        "md,me->de", mesh_normed, query_gradient, preferred_element_type=jnp.float32
    )
    mesh_normed_grad = jnp.einsum(
        "me,de->md", query_gradient, w_query, preferred_element_type=jnp.float32
    )
    mesh_grad = (
        out_grad.astype(jnp.float32)
        + normalize_back(mesh_wide, mesh_factor, gain_mesh, mesh_normed_grad)
    ).astype(jnp.bfloat16)
    local_grads = jnp.stack(
        [grad_wq, pair_grads[:, :model_width], pair_grads[:, model_width:], grad_wo]
    )
    weight_grads = lax.psum(local_grads, ("grid", "sub"))
    return (mesh_out, mesh_grad, grid_grad, weight_grads)


def solution(mesh):
    in_specs = (
        P(("grid", "sub"), None),
        P(("grid", "sub"), None),
        P(),
        P(),
        P(),
        P(),
        P(),
        P(),
        P(("grid", "sub"), None),
        P(("grid", "sub"), None),
        P(("grid", "sub"), None),
        P(("grid", "sub"), None, None, None),
        P(("grid", "sub"), None),
    )
    out_specs = (P(("grid", "sub"), None), P(("grid", "sub"), None), P(("grid", "sub"), None), P())
    return jax.shard_map(shards, mesh=mesh, in_specs=in_specs, out_specs=out_specs, check_vma=False)
```

profile of v0, /device:TPU:0, one launch (start us, length us, event | category | flops | bytes accessed | tf_op | source)
XLA Modules:
  0.0 303.4 jit_solution(8482572767754308976)
XLA Ops:
  7.2 0.0 copy-start
  7.2 3.0 copy.27
  10.2 0.5 fusion.22
  10.7 0.1 eq.39
  10.8 2.0 fusion.35
  12.8 0.9 copy-done.9
  13.7 0.9 copy.28
  14.6 6.3 %all-to-all-start = ((bf16[3,4,64,512]{3,2,0,1:T(8,128)(2,1)}), bf16[3,4,64,512]{3,2,0,1:T(8,128)(2,1)S(1)}, u32[]{:S(2)}, u32[]{:S(2)}) async-start(bf16[3,4,64,512]{3,2,0,1:T(8,128)(2,1)} %copy.28), calls=%async_computation | async-start | bytes 1572864 | tf_op jit(solution)/shard_map/all_to_all | solution.py:63
  20.9 0.1 fusion.60
  21.1 1.9 constant_dynamic-update-slice_fusion.1
  23.0 0.5 multiply_multiply_fusion.1
  23.5 0.3 convolution_convert_fusion.3
  23.8 0.2 fusion.43
  24.1 0.0 copy-done.21
  24.1 17.0 %all-to-all-done = bf16[3,4,64,512]{3,2,0,1:T(8,128)(2,1)S(1)} async-done(((bf16[3,4,64,512]{3,2,0,1:T(8,128)(2,1)}), bf16[3,4,64,512]{3,2,0,1:T(8,128)(2,1)S(1)}, u32[]{:S(2)}, u32[]{:S(2)}) %all-to-all-start) | async-done | bytes 786464 | tf_op jit(solution)/shard_map/all_to_all | solution.py:63
  41.1 0.1 fusion.91
  41.1 1.3 collective-permute-start
  42.4 3.2 %collective-permute-start.1 = (bf16[256,512]{1,0:T(8,128)(2,1)S(1)}, bf16[256,512]{1,0:T(8,128)(2,1)S(1)}, u32[]{:S(2)}, u32[]{:S(2)}) collective-permute-start(bf16[256,512]{1,0:T(8,128)(2,1)S(1)} %bitcast.119), channel_id=1, source_target_pairs={{0,4},{4,8},{8,12},{12,16},{16,20},{20,24},{24,28},{1,5},{5,9},{9,... | collective-permute-start | bytes 786440 | tf_op jit(solution)/shard_map/ppermute | solution.py:13
  45.7 0.9 constant_dynamic-update-slice_fusion
  46.6 0.1 reshape.108
  46.8 2.2 fusion.123
  49.0 11.4 %fusion.7 = bf16[64,96,1024]{2,1,0:T(8,128)(2,1)S(1)} fusion(s32[64,96]{1,0:T(8,128)} %param.22, bf16[768,1024,1]{1,0,2:T(8,128)(2,1)S(1)} %fusion.123), kind=kOutput, calls=%fused_computation.12 | convolution fusion | flops 9674686464 | bytes 14180352 | tf_op jit(solution)/shard_map/gjc,ce->gje/dot_general | solution.py:77
  60.5 3.7 %slice_bitcast_fusion.1 = (bf16[64,12,4,8,128]{4,3,2,1,0:T(8,128)(2,1)S(1)}, bf16[64,12,4,8,128]{4,3,2,1,0:T(8,128)(2,1)S(1)}) fusion(bf16[64,96,1024]{2,1,0:T(8,128)(2,1)S(1)} %fusion.7), kind=kLoop, calls=%fused_computation.22 | loop fusion | bytes 25165824
  64.2 3.3 %fusion.14 = f32[64,4,1,96]{3,2,1,0:T(1,128)S(1)} fusion(bf16[64,4,128,1]{2,3,1,0:T(2,128)(2,1)S(1)} %reshape.124, bf16[64,12,4,8,128]{4,3,2,1,0:T(8,128)(2,1)S(1)} %get-tuple-element.16), kind=kOutput, calls=%fused_computation.19 | convolution fusion | flops 6291456 | bytes 6455296 | tf_op jit(solution)/shard_map/gip,gjip->gij/dot_general | solution.py:87
  67.6 3.3 %fusion.8 = f32[64,4,1,96]{3,2,1,0:T(1,128)S(1)} fusion(bf16[64,4,128,1]{2,3,1,0:T(2,128)(2,1)S(1)} %reshape.126, bf16[64,12,4,8,128]{4,3,2,1,0:T(8,128)(2,1)S(1)} %get-tuple-element.17), kind=kOutput, calls=%fused_computation.13 | convolution fusion | flops 6291456 | bytes 6455296 | tf_op jit(solution)/shard_map/gip,gjip->gij/dot_general | solution.py:110
  70.9 0.3 fusion.92
  71.2 3.6 %fusion.39 = bf16[64,4,768]{2,1,0:T(4,128)(2,1)S(1)} fusion(s32[64,96]{1,0:T(8,128)S(1)} %copy-done.29, f32[64,4,96]{2,1,0:T(4,128)S(1)} %get-tuple-element.33, f32[64,4]{1,0:T(8,128)S(1)} %get-tuple-element.32), kind=kOutput, calls=%fused_computation.55 | convolution fusion | flops 42713088 | bytes 517120 | tf_op jit(solution)/shard_map/gij,gjc->gic/dot_general | solution.py:130
  74.8 0.2 multiply_reduce_fusion
  75.0 0.8 multiply_convert_fusion.1
  75.8 3.5 %fusion.38 = bf16[64,4,768]{2,1,0:T(4,128)(2,1)S(1)} fusion(bf16[64,4,96]{2,1,0:T(4,128)(2,1)S(1)} %get-tuple-element.26, s32[64,96]{1,0:T(8,128)S(1)} %copy-done.29), kind=kOutput, calls=%fused_computation.54 | convolution fusion | flops 42663936 | bytes 466944 | tf_op jit(solution)/shard_map/gij,gjc->gic/dot_general | solution.py:127
  79.3 0.4 convolution_convert_fusion.2
  79.8 0.3 copy.33
  80.1 0.4 convolution_convert_fusion.1
  80.5 0.3 copy.34
  80.8 0.2 fusion.56
  81.0 5.0 %collective-permute-start.2 = (bf16[256,1024]{1,0:T(8,128)(2,1)S(1)}, bf16[256,1024]{1,0:T(8,128)(2,1)S(1)}, u32[]{:S(2)}, u32[]{:S(2)}) collective-permute-start(bf16[256,1024]{1,0:T(8,128)(2,1)S(1)} %get-tuple-element.20), channel_id=1, source_target_pairs={{0,4},{4,8},{8,12},{12,16},{16,20},{20,24},{24,28},{1,5},{5,9},{9,... | collective-permute-start | bytes 1572872 | tf_op jit(solution)/shard_map/ppermute | solution.py:13
  86.0 1.3 collective-permute-start.3
  87.3 0.2 collective-permute-done.2
  87.5 4.3 %collective-permute-done.3 = bf16[256,1024]{1,0:T(8,128)(2,1)S(1)} collective-permute-done((bf16[256,1024]{1,0:T(8,128)(2,1)S(1)}, bf16[256,1024]{1,0:T(8,128)(2,1)S(1)}, u32[]{:S(2)}, u32[]{:S(2)}) %collective-permute-start.3) | collective-permute-done | bytes 524320 | tf_op jit(solution)/shard_map/ppermute | solution.py:13
  91.7 0.2 pad_maximum_fusion.1
  91.9 1.3 copy.35
  93.2 4.4 %all-to-all-start.1 = ((bf16[3,4,64,1024]{3,2,0,1:T(8,128)(2,1)}), bf16[3,4,64,1024]{3,2,0,1:T(8,128)(2,1)}, u32[]{:S(2)}, u32[]{:S(2)}) async-start(bf16[3,4,64,1024]{3,2,0,1:T(8,128)(2,1)} %copy.35), calls=%async_computation.1 | async-start | bytes 3145728 | tf_op jit(solution)/shard_map/all_to_all | solution.py:152
  97.6 0.3 all-reduce.2.cloned.1.call-start
  97.9 4.7 %fusion.10 = f32[64,4,1,128]{3,2,1,0:T(1,128)S(1)} fusion(bf16[64,12,4,8,128]{4,3,2,1,0:T(8,128)(2,1)} %copy-done.2, bf16[64,4,96,1]{2,1,0,3:T(4,128)(2,1)S(1)} %copy-done.16), kind=kOutput, calls=%fused_computation.15 | convolution fusion | flops 6291456 | bytes 6471680 | tf_op jit(solution)/shard_map/gij,gjik->gik/dot_general | solution.py:96
  102.6 1.3 convolution_bitcast_fusion
  103.9 1.7 fusion.12
  105.7 0.4 convolution_bitcast_fusion.1
  106.1 0.4 fusion.67
  106.5 24.3 %all-to-all-done.1 = bf16[3,4,64,1024]{3,2,0,1:T(8,128)(2,1)} async-done(((bf16[3,4,64,1024]{3,2,0,1:T(8,128)(2,1)}), bf16[3,4,64,1024]{3,2,0,1:T(8,128)(2,1)}, u32[]{:S(2)}, u32[]{:S(2)}) %all-to-all-start.1) | async-done | bytes 1572896 | tf_op jit(solution)/shard_map/all_to_all | solution.py:152
  130.8 1.6 copy.36
  132.4 1.0 fusion.94
  133.4 0.2 slice_bitcast_fusion.3
  133.6 0.6 copy-done.5
  134.2 2.5 pad_maximum_fusion
  136.6 0.0 all-reduce.2.cloned.1.call-update
  136.7 0.6 copy-done.23
  137.3 0.7 fusion.66
  138.0 0.8 fusion.44
  138.8 2.7 fusion.93
  141.6 6.1 %fusion.28 = (f32[2048]{0:T(1024)S(1)}, f32[2048,512]{0,1:T(8,128)S(1)}) fusion(bf16[2048,512]{0,1:T(8,128)(2,1)S(1)} %copy-done.4, f32[512]{0:T(512)S(1)} %copy-done.27, f32[768,512]{1,0:T(8,128)S(1)} %fusion.93, s32[768]{0:T(1024)S(1)} %copy-done.25), kind=kOutput, calls=%fused_computation.36 | convolution fusion | flops 9669441536 | bytes 7877632 | tf_op jit(solution)/shard_map/sp,sd->pd/dot_general | solution.py:157
  147.7 2.6 fusion.27
  150.3 3.9 %copy.37 = bf16[2048,512]{1,0:T(8,128)(2,1)} copy(bf16[2048,512]{0,1:T(8,128)(2,1)} %fusion.27) | data formatting | bytes 4194304
  154.2 137.7 %all-reduce.2.cloned.1.call-done = f32[4,512,512]{2,1,0:T(8,128)} async-done(((f32[4,512,512]{2,1,0:T(8,128)}), f32[4,512,512]{2,1,0:T(8,128)}) %all-reduce.2.cloned.1.call-update) | async-done | bytes 4194320 | tf_op jit(solution)/shard_map/psum | solution.py:178
  291.9 4.6 %copy.106 = f32[4,512,512]{2,1,0:T(8,128)} copy(f32[4,512,512]{2,1,0:T(8,128)} %all-reduce.2.cloned.1.call-done) | data formatting | bytes 8388608
  (70 shorter events, 0.3 us)
Async XLA Ops:
  7.2 16.6 %copy-start = (bf16[512,512]{1,0:T(8,128)(2,1)S(1)}, bf16[512,512]{1,0:T(8,128)(2,1)}, u32[]{:S(2)}) copy-start(bf16[512,512]{1,0:T(8,128)(2,1)} %param.17) | copy-start | bytes 1572868
  7.2 3.5 %copy-start.20 = (s32[1,3,4,64]{3,2,1,0:T(4,128)S(1)}, s32[1,3,4,64]{3,2,1,0:T(4,128)}, u32[]{:S(2)}) copy-start(s32[1,3,4,64]{3,2,1,0:T(4,128)} %param.24) | copy-start | bytes 9220
  7.2 3.6 %copy-start.26 = (f32[512]{0:T(512)S(1)}, f32[512]{0:T(512)}, u32[]{:S(2)}) copy-start(f32[512]{0:T(512)} %param.15) | copy-start | bytes 6148
  10.2 2.5 copy-start.3
  10.8 2.0 copy-start.24
  10.8 10.2 %copy-start.6 = (bf16[64,512]{1,0:T(8,128)(2,1)S(1)}, bf16[64,512]{1,0:T(8,128)(2,1)}, u32[]{:S(2)}) copy-start(bf16[64,512]{1,0:T(8,128)(2,1)} %param.14) | copy-start | bytes 196612
  12.7 0.9 copy-start.9
  12.8 10.7 %copy-start.7 = (bf16[512,512]{1,0:T(8,128)(2,1)S(1)}, bf16[512,512]{1,0:T(8,128)(2,1)}, u32[]{:S(2)}) copy-start(bf16[512,512]{1,0:T(8,128)(2,1)} %param.20) | copy-start | bytes 1572868
  12.8 10.7 %copy-start.11 = (bf16[64,512]{1,0:T(8,128)(2,1)S(1)}, bf16[64,512]{1,0:T(8,128)(2,1)}, u32[]{:S(2)}) copy-start(bf16[64,512]{1,0:T(8,128)(2,1)} %param.25) | copy-start | bytes 196612
  13.7 10.1 %copy-start.18 = (f32[512]{0:T(512)S(1)}, f32[512]{0:T(512)}, u32[]{:S(2)}) copy-start(f32[512]{0:T(512)} %param.16) | copy-start | bytes 6148
  13.7 32.0 %copy-start.12 = (bf16[512,512]{1,0:T(8,128)(2,1)S(1)}, bf16[512,512]{1,0:T(8,128)(2,1)}, u32[]{:S(2)}) copy-start(bf16[512,512]{1,0:T(8,128)(2,1)} %param.19) | copy-start | bytes 1572868
  13.7 32.9 %copy-start.13 = (f32[64,384]{1,0:T(8,128)S(1)}, f32[64,384]{1,0:T(8,128)}, u32[]{:S(2)}) copy-start(f32[64,384]{1,0:T(8,128)} %param.21) | copy-start | bytes 294916
  13.7 33.1 %copy-start.17 = (s32[64,96]{1,0:T(8,128)S(1)}, s32[64,96]{1,0:T(8,128)}, u32[]{:S(2)}) copy-start(s32[64,96]{1,0:T(8,128)} %param.23) | copy-start | bytes 73732
  14.6 26.5 %all-to-all-start = ((bf16[3,4,64,512]{3,2,0,1:T(8,128)(2,1)}), bf16[3,4,64,512]{3,2,0,1:T(8,128)(2,1)S(1)}, u32[]{:S(2)}, u32[]{:S(2)}) async-start(bf16[3,4,64,512]{3,2,0,1:T(8,128)(2,1)} %copy.28), calls=%async_computation | async-start | bytes 1572864 | tf_op jit(solution)/shard_map/all_to_all | solution.py:63
  23.5 0.6 copy-start.21
  41.1 5.7 %collective-permute-start = (bf16[256,512]{1,0:T(8,128)(2,1)S(1)}, bf16[256,512]{1,0:T(8,128)(2,1)S(1)}, u32[]{:S(2)}, u32[]{:S(2)}) collective-permute-start(bf16[256,512]{1,0:T(8,128)(2,1)S(1)} %bitcast.120), channel_id=1, source_target_pairs={{4,0},{8,4},{12,8},{16,12},{20,16},{24,20},{28,24},{5,1},{9,5},{13... | collective-permute-start | bytes 786440 | tf_op jit(solution)/shard_map/ppermute | solution.py:13
  42.4 4.4 %collective-permute-start.1 = (bf16[256,512]{1,0:T(8,128)(2,1)S(1)}, bf16[256,512]{1,0:T(8,128)(2,1)S(1)}, u32[]{:S(2)}, u32[]{:S(2)}) collective-permute-start(bf16[256,512]{1,0:T(8,128)(2,1)S(1)} %bitcast.119), channel_id=1, source_target_pairs={{0,4},{4,8},{8,12},{12,16},{16,20},{20,24},{24,28},{1,5},{5,9},{9,... | collective-permute-start | bytes 786440 | tf_op jit(solution)/shard_map/ppermute | solution.py:13
  64.2 6.7 %copy-start.1 = (bf16[64,12,4,8,128]{4,3,2,1,0:T(8,128)(2,1)}, bf16[64,12,4,8,128]{4,3,2,1,0:T(8,128)(2,1)S(1)}, u32[]{:S(2)}) copy-start(bf16[64,12,4,8,128]{4,3,2,1,0:T(8,128)(2,1)S(1)} %get-tuple-element.16) | copy-start | bytes 18874372
  64.2 6.7 %copy-start.2 = (bf16[64,12,4,8,128]{4,3,2,1,0:T(8,128)(2,1)}, bf16[64,12,4,8,128]{4,3,2,1,0:T(8,128)(2,1)S(1)}, u32[]{:S(2)}) copy-start(bf16[64,12,4,8,128]{4,3,2,1,0:T(8,128)(2,1)S(1)} %get-tuple-element.17) | copy-start | bytes 18874372
  67.6 3.6 %copy-start.29 = (s32[64,96]{1,0:T(8,128)S(1)}, s32[64,96]{1,0:T(8,128)}, u32[]{:S(2)}) copy-start(s32[64,96]{1,0:T(8,128)} %param.22) | copy-start | bytes 73732
  75.8 4.0 %copy-start.14 = (bf16[64,4,96]{2,1,0:T(4,128)(2,1)}, bf16[64,4,96]{2,1,0:T(4,128)(2,1)S(1)}, u32[]{:S(2)}) copy-start(bf16[64,4,96]{2,1,0:T(4,128)(2,1)S(1)} %get-tuple-element.26) | copy-start | bytes 147460
  81.0 6.5 %collective-permute-start.2 = (bf16[256,1024]{1,0:T(8,128)(2,1)S(1)}, bf16[256,1024]{1,0:T(8,128)(2,1)S(1)}, u32[]{:S(2)}, u32[]{:S(2)}) collective-permute-start(bf16[256,1024]{1,0:T(8,128)(2,1)S(1)} %get-tuple-element.20), channel_id=1, source_target_pairs={{0,4},{4,8},{8,12},{12,16},{16,20},{20,24},{24,28},{1,5},{5,9},{9,... | collective-permute-start | bytes 1572872 | tf_op jit(solution)/shard_map/ppermute | solution.py:13
  86.0 5.8 %collective-permute-start.3 = (bf16[256,1024]{1,0:T(8,128)(2,1)S(1)}, bf16[256,1024]{1,0:T(8,128)(2,1)S(1)}, u32[]{:S(2)}, u32[]{:S(2)}) collective-permute-start(bf16[256,1024]{1,0:T(8,128)(2,1)S(1)} %get-tuple-element.21), channel_id=1, source_target_pairs={{4,0},{8,4},{12,8},{16,12},{20,16},{24,20},{28,24},{5,1},{9,5},{13... | collective-permute-start | bytes 1572872 | tf_op jit(solution)/shard_map/ppermute | solution.py:13
  91.7 6.1 %copy-start.16 = (bf16[64,4,96,1]{2,1,0,3:T(4,128)(2,1)S(1)}, bf16[64,4,96,1]{2,1,0,3:T(4,128)(2,1)}, u32[]{:S(2)}) copy-start(bf16[64,4,96,1]{2,1,0,3:T(4,128)(2,1)} %get-tuple-element.27) | copy-start | bytes 147460
  91.9 12.0 %slice-start = ((s8[6291456]{0:T(1024)(128)(4,1)}), s8[2097152]{0:T(1024)(128)(4,1)S(1)}, s32[]{:S(2)}) async-start(s8[6291456]{0:T(1024)(128)(4,1)} %bitcast.102), calls=%async_computation.3 | async-start | bytes 4194304
  93.2 37.6 %all-to-all-start.1 = ((bf16[3,4,64,1024]{3,2,0,1:T(8,128)(2,1)}), bf16[3,4,64,1024]{3,2,0,1:T(8,128)(2,1)}, u32[]{:S(2)}, u32[]{:S(2)}) async-start(bf16[3,4,64,1024]{3,2,0,1:T(8,128)(2,1)} %copy.35), calls=%async_computation.1 | async-start | bytes 3145728 | tf_op jit(solution)/shard_map/all_to_all | solution.py:152
  97.6 194.4 %all-reduce.2.cloned.1.call-start = ((), (), s32[]{:S(2)}) async-start(), calls=%async_computation.2 | async-start | bytes 8388608 | tf_op jit(solution)/shard_map/psum | solution.py:178
  97.8 6.0 %copy-start.15 = (bf16[64,4,96]{2,1,0:T(4,128)(2,1)S(1)}, bf16[64,4,96]{2,1,0:T(4,128)(2,1)}, u32[]{:S(2)}) copy-start(bf16[64,4,96]{2,1,0:T(4,128)(2,1)} %copy-done.14) | copy-start | bytes 147460
  97.9 6.0 %slice-start.1 = ((s8[6291456]{0:T(1024)(128)(4,1)}), s8[4194304]{0:T(1024)(128)(4,1)S(1)}, s32[]{:S(2)}) async-start(s8[6291456]{0:T(1024)(128)(4,1)} %bitcast.102), calls=%async_computation.4 | async-start | bytes 8388608
  102.5 3.1 %copy-start.19 = (f32[512]{0:T(512)S(1)}, f32[512]{0:T(512)}, u32[]{:S(2)}) copy-start(f32[512]{0:T(512)} %param.16) | copy-start | bytes 6148
  102.5 3.1 %copy-start.22 = (f32[64]{0:T(128)S(1)}, f32[64]{0:T(128)}, u32[]{:S(2)}) copy-start(f32[64]{0:T(128)} %copy-done.21) | copy-start | bytes 772
  105.6 26.8 %copy-start.10 = (bf16[768,512]{1,0:T(8,128)(2,1)S(1)}, bf16[768,512]{1,0:T(8,128)(2,1)}, u32[]{:S(2)}) copy-start(bf16[768,512]{1,0:T(8,128)(2,1)} %copy-done.9) | copy-start | bytes 2359300
  132.4 1.3 copy-start.8
  132.4 1.8 copy-start.5
  136.6 0.7 copy-start.23
  136.6 0.7 copy-start.28
  136.6 4.9 %copy-start.4 = (bf16[2048,512]{0,1:T(8,128)(2,1)S(1)}, bf16[2048,512]{0,1:T(8,128)(2,1)}, u32[]{:S(2)}) copy-start(bf16[2048,512]{0,1:T(8,128)(2,1)} %copy-done.3) | copy-start | bytes 6291460
  136.6 4.9 %copy-start.25 = (s32[768]{0:T(1024)S(1)}, s32[768]{0:T(1024)}, u32[]{:S(2)}) copy-start(s32[768]{0:T(1024)} %copy-done.24) | copy-start | bytes 9220
  136.6 4.9 %copy-start.27 = (f32[512]{0:T(512)S(1)}, f32[512]{0:T(512)}, u32[]{:S(2)}) copy-start(f32[512]{0:T(512)} %param.15) | copy-start | bytes 6148
Sparse Core Ops, SparseCore 0:
  136.8 155.1 all-reduce.1
where the time goes:
time: 304 us; the launch traced here: 303 us
  waiting for transfers between devices  184 us (61%)
  matrix products  49.8 us (16%)
  local copies, waits for them, and re-layouts  25.1 us (8%)
  starting transfers between devices  21.8 us (7%)
  between operations  14.6 us (5%)
  other arithmetic  8.64 us (3%)
    psum x1, waiting for transfers between devices, shards(): weight_grads = lax.psum(local_grads, ('grid', 'sub'))  138 us
    all_to_all x1, waiting for transfers between devices, shards(): lax.all_to_all(home, 'sub', split_axis=1, concat_axis=1, tiled=True)  24.3 us
    unnamed x69, local copies, waits for them, and re-layouts  19.4 us
    all_to_all x1, waiting for transfers between devices, shards(): lax.all_to_all(packet, 'sub', split_axis=1, concat_axis=1, tiled=True)  17 us
    dot_general x1, matrix products, shards(): jnp.einsum('gjc,ce->gje', slot_onehot, recv_pair, preferred_element_type=...  11.4 us
    ppermute x4, starting transfers between devices, from_behind(): return lax.ppermute(block, axis, route)  10.8 us
    all_to_all x1, starting transfers between devices, shards(): lax.all_to_all(packet, 'sub', split_axis=1, concat_axis=1, tiled=True)  6.35 us
    dot_general x1, matrix products, shards(): jnp.einsum('sp,sd->pd', send_match.astype(jnp.float32), slot_back, precis...  6.08 us
  transfers between devices with their start and end apart: 7, of which 5 were waited for; matrix products, arithmetic and copies ran while one was open for 10% of the time, Pallas kernels for 0%

commit v1 on v0

--- a/solution.py
+++ b/solution.py
@@ -60,9 +60,10 @@
     )
     packet = sent_normed.reshape(3, sub_count, slots_per, model_width)
     packet_width = packet.shape[3]
-    mixed = lax.all_to_all(packet, "sub", split_axis=1, concat_axis=1, tiled=True).reshape(
-        3, block, packet_width
-    )
+    mixed = jnp.concatenate(
+        lax.all_to_all(jnp.stack(jnp.split(packet, lax.axis_size("sub"), axis=1)), "sub", 0, 0),
+        axis=1,
+    ).reshape(3, block, packet_width)
     pieces = []
     for offset in (0, 1, 2):
         piece = mixed[offset]

time: 304 us -> 308 us (1.013)
    unnamed x69 -> x65, local copies, waits for them, and re-layouts: 19.4 us -> 19.4 us
where the time goes in v1:
time: 308 us; the launch traced here: 307 us
  waiting for transfers between devices  185 us (60%)
  matrix products  52.6 us (17%)
  local copies, waits for them, and re-layouts  25.1 us (8%)
  starting transfers between devices  20.2 us (7%)
  between operations  14.5 us (5%)
  other arithmetic  10.4 us (3%)
    psum x1, waiting for transfers between devices, shards(): weight_grads = lax.psum(local_grads, ('grid', 'sub'))  138 us
    all_to_all x1, waiting for transfers between devices, shards(): lax.all_to_all(home, 'sub', split_axis=1, concat_axis=1, tiled=True)  24.3 us
    unnamed x65, local copies, waits for them, and re-layouts  19.4 us
    all_to_all x1, waiting for transfers between devices, shards(): lax.all_to_all(jnp.stack(jnp.split(packet, lax.axis_size('sub'), axis=1))...  18.1 us
    dot_general x1, matrix products, shards(): jnp.einsum('gjc,ce->gje', slot_onehot, recv_pair, preferred_element_type=...  11.4 us
    ppermute x4, starting transfers between devices, from_behind(): return lax.ppermute(block, axis, route)  9.18 us
    all_to_all x1, starting transfers between devices, shards(): lax.all_to_all(jnp.stack(jnp.split(packet, lax.axis_size('sub'), axis=1))...  6.34 us
  transfers between devices with their start and end apart: 7, of which 5 were waited for; matrix products, arithmetic and copies ran while one was open for 10% of the time, Pallas kernels for 0%

profile of v1, /device:TPU:0, one launch (start us, length us, event | category | flops | bytes accessed | tf_op | source)
XLA Modules:
  0.0 307.5 jit_solution(14866794466971552783)
XLA Ops:
  7.2 3.0 copy.33
  10.2 0.5 fusion.22
  10.7 0.1 eq.39
  10.8 2.0 fusion.35
  12.8 0.9 copy-done.8
  13.7 0.1 slice_bitcast_fusion.7
  13.7 1.0 pad_maximum_fusion.2
  14.7 6.3 %all-to-all-start = ((bf16[4,3,1,64,512]{4,3,1,2,0:T(8,128)(2,1)}), bf16[4,3,1,64,512]{4,3,1,2,0:T(8,128)(2,1)S(1)}, u32[]{:S(2)}, u32[]{:S(2)}) async-start(bf16[4,3,1,64,512]{4,3,1,2,0:T(8,128)(2,1)} %pad_maximum_fusion.2), calls=%async_computation | async-start | bytes 1572864 | tf_op jit(solution)/shard_map/all_to_all | solution.py:64
  21.1 0.1 fusion.60
  21.2 0.9 constant_dynamic-update-slice_fusion.1
  22.0 0.5 multiply_multiply_fusion.1
  22.5 0.3 convolution_convert_fusion.3
  22.8 0.2 fusion.43
  23.1 18.1 %all-to-all-done = bf16[4,3,1,64,512]{4,3,1,2,0:T(8,128)(2,1)S(1)} async-done(((bf16[4,3,1,64,512]{4,3,1,2,0:T(8,128)(2,1)}), bf16[4,3,1,64,512]{4,3,1,2,0:T(8,128)(2,1)S(1)}, u32[]{:S(2)}, u32[]{:S(2)}) %all-to-all-start) | async-done | bytes 786464 | tf_op jit(solution)/shard_map/all_to_all | solution.py:64
  41.2 0.1 fusion.91
  41.2 1.3 collective-permute-start
  42.5 3.2 %collective-permute-start.1 = (bf16[256,512]{1,0:T(8,128)(2,1)S(1)}, bf16[256,512]{1,0:T(8,128)(2,1)S(1)}, u32[]{:S(2)}, u32[]{:S(2)}) collective-permute-start(bf16[256,512]{1,0:T(8,128)(2,1)S(1)} %bitcast.135), channel_id=1, source_target_pairs={{0,4},{4,8},{8,12},{12,16},{16,20},{20,24},{24,28},{1,5},{5,9},{9,... | collective-permute-start | bytes 786440 | tf_op jit(solution)/shard_map/ppermute | solution.py:13
  45.8 0.9 constant_dynamic-update-slice_fusion
  46.7 1.0 reshape.111
  47.7 0.8 broadcast_compare_fusion
  48.5 2.2 fusion.123
  50.7 11.4 %fusion.7 = bf16[64,96,1024]{2,1,0:T(8,128)(2,1)S(1)} fusion(s32[64,96]{1,0:T(8,128)} %param.22, bf16[768,1024,1]{1,0,2:T(8,128)(2,1)S(1)} %fusion.123), kind=kOutput, calls=%fused_computation.12 | convolution fusion | flops 9674686464 | bytes 14180352 | tf_op jit(solution)/shard_map/gjc,ce->gje/dot_general | solution.py:78
  62.2 4.9 %slice_bitcast_fusion.1 = (bf16[64,12,4,8,128]{4,3,2,1,0:T(8,128)(2,1)S(1)}, bf16[64,12,4,8,128]{4,3,2,1,0:T(8,128)(2,1)}) fusion(bf16[64,96,1024]{2,1,0:T(8,128)(2,1)S(1)} %fusion.7), kind=kLoop, calls=%fused_computation.22 | loop fusion | bytes 25165824
  67.1 3.3 %fusion.14 = f32[64,4,1,96]{3,2,1,0:T(1,128)S(1)} fusion(bf16[64,4,128,1]{2,3,1,0:T(2,128)(2,1)S(1)} %reshape.127, bf16[64,12,4,8,128]{4,3,2,1,0:T(8,128)(2,1)S(1)} %get-tuple-element.16), kind=kOutput, calls=%fused_computation.19 | convolution fusion | flops 6291456 | bytes 6455296 | tf_op jit(solution)/shard_map/gip,gjip->gij/dot_general | solution.py:88
  70.4 0.3 fusion.92
  70.7 3.6 %fusion.39 = bf16[64,4,768]{2,1,0:T(4,128)(2,1)S(1)} fusion(s32[64,96]{1,0:T(8,128)S(1)} %copy-done.27, f32[64,4,96]{2,1,0:T(4,128)S(1)} %get-tuple-element.37, f32[64,4]{1,0:T(8,128)S(1)} %get-tuple-element.36), kind=kOutput, calls=%fused_computation.55 | convolution fusion | flops 42713088 | bytes 517120 | tf_op jit(solution)/shard_map/gij,gjc->gic/dot_general | solution.py:131
  74.3 0.4 convolution_convert_fusion.1
  74.7 0.3 copy.42
  75.0 6.1 %fusion.8 = f32[64,4,1,96]{3,2,1,0:T(1,128)S(1)} fusion(bf16[64,4,128,1]{2,3,1,0:T(2,128)(2,1)S(1)} %reshape.129, bf16[64,12,4,8,128]{4,3,2,1,0:T(8,128)(2,1)} %get-tuple-element.17), kind=kOutput, calls=%fused_computation.13 | convolution fusion | flops 6291456 | bytes 6455296 | tf_op jit(solution)/shard_map/gip,gjip->gij/dot_general | solution.py:111
  81.1 0.3 multiply_reduce_fusion
  81.4 0.8 multiply_convert_fusion.1
  82.2 3.5 %fusion.38 = bf16[64,4,768]{2,1,0:T(4,128)(2,1)S(1)} fusion(bf16[64,4,96]{2,1,0:T(4,128)(2,1)S(1)} %get-tuple-element.30, s32[64,96]{1,0:T(8,128)S(1)} %copy-done.27), kind=kOutput, calls=%fused_computation.54 | convolution fusion | flops 42663936 | bytes 466944 | tf_op jit(solution)/shard_map/gij,gjc->gic/dot_general | solution.py:128
  85.7 0.4 convolution_convert_fusion.2
  86.1 0.3 copy.41
  86.4 0.2 fusion.56
  86.6 3.4 %collective-permute-start.2 = (bf16[256,1024]{1,0:T(8,128)(2,1)S(1)}, bf16[256,1024]{1,0:T(8,128)(2,1)S(1)}, u32[]{:S(2)}, u32[]{:S(2)}) collective-permute-start(bf16[256,1024]{1,0:T(8,128)(2,1)S(1)} %get-tuple-element.20), channel_id=1, source_target_pairs={{0,4},{4,8},{8,12},{12,16},{16,20},{20,24},{24,28},{1,5},{5,9},{9,... | collective-permute-start | bytes 1572872 | tf_op jit(solution)/shard_map/ppermute | solution.py:13
  90.0 1.3 collective-permute-start.3
  91.3 0.2 collective-permute-done.2
  91.5 4.3 %collective-permute-done.3 = bf16[256,1024]{1,0:T(8,128)(2,1)S(1)} collective-permute-done((bf16[256,1024]{1,0:T(8,128)(2,1)S(1)}, bf16[256,1024]{1,0:T(8,128)(2,1)S(1)}, u32[]{:S(2)}, u32[]{:S(2)}) %collective-permute-start.3) | collective-permute-done | bytes 524320 | tf_op jit(solution)/shard_map/ppermute | solution.py:13
  95.7 0.2 pad_maximum_fusion.1
  95.9 1.3 copy.43
  97.2 4.4 %all-to-all-start.1 = ((bf16[3,4,64,1024]{3,2,0,1:T(8,128)(2,1)}), bf16[3,4,64,1024]{3,2,0,1:T(8,128)(2,1)}, u32[]{:S(2)}, u32[]{:S(2)}) async-start(bf16[3,4,64,1024]{3,2,0,1:T(8,128)(2,1)} %copy.43), calls=%async_computation.1 | async-start | bytes 3145728 | tf_op jit(solution)/shard_map/all_to_all | solution.py:153
  101.6 0.3 all-reduce.2.cloned.1.call-start
  101.9 4.7 %fusion.10 = f32[64,4,1,128]{3,2,1,0:T(1,128)S(1)} fusion(bf16[64,12,4,8,128]{4,3,2,1,0:T(8,128)(2,1)} %get-tuple-element.17, bf16[64,4,96,1]{2,1,0,3:T(4,128)(2,1)S(1)} %copy-done.15), kind=kOutput, calls=%fused_computation.15 | convolution fusion | flops 6291456 | bytes 6471680 | tf_op jit(solution)/shard_map/gij,gjik->gik/dot_general | solution.py:97
  106.6 1.3 convolution_bitcast_fusion
  107.9 1.7 fusion.12
  109.7 0.4 convolution_bitcast_fusion.1
  110.1 0.4 fusion.67
  110.5 24.3 %all-to-all-done.1 = bf16[3,4,64,1024]{3,2,0,1:T(8,128)(2,1)} async-done(((bf16[3,4,64,1024]{3,2,0,1:T(8,128)(2,1)}), bf16[3,4,64,1024]{3,2,0,1:T(8,128)(2,1)}, u32[]{:S(2)}, u32[]{:S(2)}) %all-to-all-start.1) | async-done | bytes 1572896 | tf_op jit(solution)/shard_map/all_to_all | solution.py:153
  134.8 1.6 copy.44
  136.4 1.0 fusion.94
  137.4 0.2 slice_bitcast_fusion.3
  137.7 0.6 copy-done.4
  138.2 2.5 pad_maximum_fusion
  140.7 0.0 all-reduce.2.cloned.1.call-update
  140.7 0.6 copy-done.21
  141.3 0.7 fusion.66
  142.0 0.8 fusion.44
  142.8 2.7 fusion.93
  145.6 6.1 %fusion.28 = (f32[2048]{0:T(1024)S(1)}, f32[2048,512]{0,1:T(8,128)S(1)}) fusion(bf16[2048,512]{0,1:T(8,128)(2,1)S(1)} %copy-done.3, f32[512]{0:T(512)S(1)} %copy-done.25, f32[768,512]{1,0:T(8,128)S(1)} %fusion.93, s32[768]{0:T(1024)S(1)} %copy-done.23), kind=kOutput, calls=%fused_computation.36 | convolution fusion | flops 9669441536 | bytes 7877632 | tf_op jit(solution)/shard_map/sp,sd->pd/dot_general | solution.py:158
  151.7 2.6 fusion.27
  154.3 3.9 %copy.45 = bf16[2048,512]{1,0:T(8,128)(2,1)} copy(bf16[2048,512]{0,1:T(8,128)(2,1)} %fusion.27) | data formatting | bytes 4194304
  158.2 137.8 %all-reduce.2.cloned.1.call-done = f32[4,512,512]{2,1,0:T(8,128)} async-done(((f32[4,512,512]{2,1,0:T(8,128)}), f32[4,512,512]{2,1,0:T(8,128)}) %all-reduce.2.cloned.1.call-update) | async-done | bytes 4194320 | tf_op jit(solution)/shard_map/psum | solution.py:179
  296.0 4.6 %copy.117 = f32[4,512,512]{2,1,0:T(8,128)} copy(f32[4,512,512]{2,1,0:T(8,128)} %all-reduce.2.cloned.1.call-done) | data formatting | bytes 8388608
  (67 shorter events, 0.3 us)
Async XLA Ops:
  7.2 15.7 %copy-start = (bf16[512,512]{1,0:T(8,128)(2,1)S(1)}, bf16[512,512]{1,0:T(8,128)(2,1)}, u32[]{:S(2)}) copy-start(bf16[512,512]{1,0:T(8,128)(2,1)} %param.17) | copy-start | bytes 1572868
  7.2 3.5 %copy-start.18 = (s32[1,3,4,64]{3,2,1,0:T(4,128)S(1)}, s32[1,3,4,64]{3,2,1,0:T(4,128)}, u32[]{:S(2)}) copy-start(s32[1,3,4,64]{3,2,1,0:T(4,128)} %param.24) | copy-start | bytes 9220
  7.2 3.6 %copy-start.24 = (f32[512]{0:T(512)S(1)}, f32[512]{0:T(512)}, u32[]{:S(2)}) copy-start(f32[512]{0:T(512)} %param.15) | copy-start | bytes 6148
  10.2 2.5 copy-start.2
  10.8 2.0 copy-start.22
  12.7 0.9 copy-start.8
  12.8 8.3 %copy-start.5 = (bf16[64,512]{1,0:T(8,128)(2,1)S(1)}, bf16[64,512]{1,0:T(8,128)(2,1)}, u32[]{:S(2)}) copy-start(bf16[64,512]{1,0:T(8,128)(2,1)} %param.14) | copy-start | bytes 196612
  12.8 9.8 %copy-start.6 = (bf16[512,512]{1,0:T(8,128)(2,1)S(1)}, bf16[512,512]{1,0:T(8,128)(2,1)}, u32[]{:S(2)}) copy-start(bf16[512,512]{1,0:T(8,128)(2,1)} %param.20) | copy-start | bytes 1572868
  12.8 9.8 %copy-start.10 = (bf16[64,512]{1,0:T(8,128)(2,1)S(1)}, bf16[64,512]{1,0:T(8,128)(2,1)}, u32[]{:S(2)}) copy-start(bf16[64,512]{1,0:T(8,128)(2,1)} %param.25) | copy-start | bytes 196612
  13.7 7.5 %copy-start.11 = (bf16[512,512]{1,0:T(8,128)(2,1)S(1)}, bf16[512,512]{1,0:T(8,128)(2,1)}, u32[]{:S(2)}) copy-start(bf16[512,512]{1,0:T(8,128)(2,1)} %param.18) | copy-start | bytes 1572868
  13.7 9.2 %copy-start.16 = (f32[512]{0:T(512)S(1)}, f32[512]{0:T(512)}, u32[]{:S(2)}) copy-start(f32[512]{0:T(512)} %param.16) | copy-start | bytes 6148
  13.7 32.1 %copy-start.12 = (bf16[512,512]{1,0:T(8,128)(2,1)S(1)}, bf16[512,512]{1,0:T(8,128)(2,1)}, u32[]{:S(2)}) copy-start(bf16[512,512]{1,0:T(8,128)(2,1)} %param.19) | copy-start | bytes 1572868
  14.7 26.5 %all-to-all-start = ((bf16[4,3,1,64,512]{4,3,1,2,0:T(8,128)(2,1)}), bf16[4,3,1,64,512]{4,3,1,2,0:T(8,128)(2,1)S(1)}, u32[]{:S(2)}, u32[]{:S(2)}) async-start(bf16[4,3,1,64,512]{4,3,1,2,0:T(8,128)(2,1)} %pad_maximum_fusion.2), calls=%async_computation | async-start | bytes 1572864 | tf_op jit(solution)/shard_map/all_to_all | solution.py:64
  22.5 18.6 %copy-start.19 = (f32[64]{0:T(128)}, f32[64]{0:T(128)S(1)}, u32[]{:S(2)}) copy-start(f32[64]{0:T(128)S(1)} %get-tuple-element.35) | copy-start | bytes 772
  41.2 7.3 %collective-permute-start = (bf16[256,512]{1,0:T(8,128)(2,1)S(1)}, bf16[256,512]{1,0:T(8,128)(2,1)S(1)}, u32[]{:S(2)}, u32[]{:S(2)}) collective-permute-start(bf16[256,512]{1,0:T(8,128)(2,1)S(1)} %bitcast.136), channel_id=1, source_target_pairs={{4,0},{8,4},{12,8},{16,12},{20,16},{24,20},{28,24},{5,1},{9,5},{13... | collective-permute-start | bytes 786440 | tf_op jit(solution)/shard_map/ppermute | solution.py:13
  42.5 6.0 %collective-permute-start.1 = (bf16[256,512]{1,0:T(8,128)(2,1)S(1)}, bf16[256,512]{1,0:T(8,128)(2,1)S(1)}, u32[]{:S(2)}, u32[]{:S(2)}) collective-permute-start(bf16[256,512]{1,0:T(8,128)(2,1)S(1)} %bitcast.135), channel_id=1, source_target_pairs={{0,4},{4,8},{8,12},{12,16},{16,20},{20,24},{24,28},{1,5},{5,9},{9,... | collective-permute-start | bytes 786440 | tf_op jit(solution)/shard_map/ppermute | solution.py:13
  67.1 7.2 %copy-start.1 = (bf16[64,12,4,8,128]{4,3,2,1,0:T(8,128)(2,1)}, bf16[64,12,4,8,128]{4,3,2,1,0:T(8,128)(2,1)S(1)}, u32[]{:S(2)}) copy-start(bf16[64,12,4,8,128]{4,3,2,1,0:T(8,128)(2,1)S(1)} %get-tuple-element.16) | copy-start | bytes 18874372
  67.1 3.6 %copy-start.27 = (s32[64,96]{1,0:T(8,128)S(1)}, s32[64,96]{1,0:T(8,128)}, u32[]{:S(2)}) copy-start(s32[64,96]{1,0:T(8,128)} %param.22) | copy-start | bytes 73732
  82.2 4.0 %copy-start.13 = (bf16[64,4,96]{2,1,0:T(4,128)(2,1)}, bf16[64,4,96]{2,1,0:T(4,128)(2,1)S(1)}, u32[]{:S(2)}) copy-start(bf16[64,4,96]{2,1,0:T(4,128)(2,1)S(1)} %get-tuple-element.30) | copy-start | bytes 147460
  86.6 4.9 %collective-permute-start.2 = (bf16[256,1024]{1,0:T(8,128)(2,1)S(1)}, bf16[256,1024]{1,0:T(8,128)(2,1)S(1)}, u32[]{:S(2)}, u32[]{:S(2)}) collective-permute-start(bf16[256,1024]{1,0:T(8,128)(2,1)S(1)} %get-tuple-element.20), channel_id=1, source_target_pairs={{0,4},{4,8},{8,12},{12,16},{16,20},{20,24},{24,28},{1,5},{5,9},{9,... | collective-permute-start | bytes 1572872 | tf_op jit(solution)/shard_map/ppermute | solution.py:13
  90.0 5.8 %collective-permute-start.3 = (bf16[256,1024]{1,0:T(8,128)(2,1)S(1)}, bf16[256,1024]{1,0:T(8,128)(2,1)S(1)}, u32[]{:S(2)}, u32[]{:S(2)}) collective-permute-start(bf16[256,1024]{1,0:T(8,128)(2,1)S(1)} %get-tuple-element.21), channel_id=1, source_target_pairs={{4,0},{8,4},{12,8},{16,12},{20,16},{24,20},{28,24},{5,1},{9,5},{13... | collective-permute-start | bytes 1572872 | tf_op jit(solution)/shard_map/ppermute | solution.py:13
  95.7 6.2 %copy-start.15 = (bf16[64,4,96,1]{2,1,0,3:T(4,128)(2,1)S(1)}, bf16[64,4,96,1]{2,1,0,3:T(4,128)(2,1)}, u32[]{:S(2)}) copy-start(bf16[64,4,96,1]{2,1,0,3:T(4,128)(2,1)} %get-tuple-element.31) | copy-start | bytes 147460
  95.9 12.0 %slice-start = ((s8[6291456]{0:T(1024)(128)(4,1)}), s8[2097152]{0:T(1024)(128)(4,1)S(1)}, s32[]{:S(2)}) async-start(s8[6291456]{0:T(1024)(128)(4,1)} %bitcast.117), calls=%async_computation.3 | async-start | bytes 4194304
  97.2 37.6 %all-to-all-start.1 = ((bf16[3,4,64,1024]{3,2,0,1:T(8,128)(2,1)}), bf16[3,4,64,1024]{3,2,0,1:T(8,128)(2,1)}, u32[]{:S(2)}, u32[]{:S(2)}) async-start(bf16[3,4,64,1024]{3,2,0,1:T(8,128)(2,1)} %copy.43), calls=%async_computation.1 | async-start | bytes 3145728 | tf_op jit(solution)/shard_map/all_to_all | solution.py:153
  101.6 194.4 %all-reduce.2.cloned.1.call-start = ((), (), s32[]{:S(2)}) async-start(), calls=%async_computation.2 | async-start | bytes 8388608 | tf_op jit(solution)/shard_map/psum | solution.py:179
  101.9 6.0 %copy-start.14 = (bf16[64,4,96]{2,1,0:T(4,128)(2,1)S(1)}, bf16[64,4,96]{2,1,0:T(4,128)(2,1)}, u32[]{:S(2)}) copy-start(bf16[64,4,96]{2,1,0:T(4,128)(2,1)} %copy-done.13) | copy-start | bytes 147460
  101.9 6.0 %slice-start.1 = ((s8[6291456]{0:T(1024)(128)(4,1)}), s8[4194304]{0:T(1024)(128)(4,1)S(1)}, s32[]{:S(2)}) async-start(s8[6291456]{0:T(1024)(128)(4,1)} %bitcast.117), calls=%async_computation.4 | async-start | bytes 8388608
  106.6 3.1 %copy-start.17 = (f32[512]{0:T(512)S(1)}, f32[512]{0:T(512)}, u32[]{:S(2)}) copy-start(f32[512]{0:T(512)} %param.16) | copy-start | bytes 6148
  106.6 3.1 %copy-start.20 = (f32[64]{0:T(128)S(1)}, f32[64]{0:T(128)}, u32[]{:S(2)}) copy-start(f32[64]{0:T(128)} %copy-done.19) | copy-start | bytes 772
  109.6 26.8 %copy-start.9 = (bf16[768,512]{1,0:T(8,128)(2,1)S(1)}, bf16[768,512]{1,0:T(8,128)(2,1)}, u32[]{:S(2)}) copy-start(bf16[768,512]{1,0:T(8,128)(2,1)} %copy-done.8) | copy-start | bytes 2359300
  136.4 1.3 copy-start.7
  136.4 1.8 copy-start.4
  140.7 0.6 copy-start.21
  140.7 0.6 copy-start.26
  140.7 4.9 %copy-start.3 = (bf16[2048,512]{0,1:T(8,128)(2,1)S(1)}, bf16[2048,512]{0,1:T(8,128)(2,1)}, u32[]{:S(2)}) copy-start(bf16[2048,512]{0,1:T(8,128)(2,1)} %copy-done.2) | copy-start | bytes 6291460
  140.7 4.9 %copy-start.23 = (s32[768]{0:T(1024)S(1)}, s32[768]{0:T(1024)}, u32[]{:S(2)}) copy-start(s32[768]{0:T(1024)} %copy-done.22) | copy-start | bytes 9220
  140.7 4.9 %copy-start.25 = (f32[512]{0:T(512)S(1)}, f32[512]{0:T(512)}, u32[]{:S(2)}) copy-start(f32[512]{0:T(512)} %param.15) | copy-start | bytes 6148
Sparse Core Ops, SparseCore 0:
  140.8 155.0 all-reduce.1
